TPU v7x, 256 devices: a whole 4x4x8 slice. The times are simulated.
256 devices in a mesh: dp: 2 (over y_hi), fsdp: 16 (over x, y_lo, core), tensor: 8 (over z).
Axes of the slice: x: 4, y: 4 (y_hi: 2, y_lo: 2; y = y_hi * 2 + y_lo), z: 8, core: 2. Of those that a mesh axis runs over, the one named last changes fastest.
Arguments:
- activations: bfloat16 [4096, 8192], P(('dp', 'fsdp'), 'tensor'), may hold values from -6 to 6
- cotangent: bfloat16 [4096, 8192], P(('dp', 'fsdp'), 'tensor'), may hold values from -6 to 6
- up_tiles: bfloat16 [1024, 128, 128], P(('fsdp', 'tensor')), may hold values from -0.1875 to 0.1875
- down_tiles: bfloat16 [1024, 128, 128], P(('fsdp', 'tensor')), may hold values from -0.125 to 0.125
- up_rows: int32 [128, 8], P(None, 'tensor'), may hold values from 0 to 63, as said below
- up_cols: int32 [128, 8], P(None, 'tensor'), may hold values from 0 to 15, as said below
- down_rows: int32 [128, 8], P(None, 'tensor'), may hold values from 0 to 15, as said below
- down_cols: int32 [128, 8], P(None, 'tensor'), may hold values from 0 to 63, as said below
Outputs:
- output: bfloat16 [4096, 8192], P(('dp', 'fsdp'), 'tensor')
- input_grad: bfloat16 [4096, 8192], P(('dp', 'fsdp'), 'tensor')
- up_grad: float32 [1024, 128, 128], P(('fsdp', 'tensor'))
- down_grad: float32 [1024, 128, 128], P(('fsdp', 'tensor'))
Inputs may be any that keep to these rules, and one draw needn't show every extreme that they name: `up_rows`: within a column, the up tiles of one hidden-unit block name distinct feature blocks. `up_cols`: every value occurs exactly 8 times in each column. `down_rows`: every value occurs exactly 8 times in each column. `down_cols`: within a column, the down tiles of one hidden-unit block name distinct feature blocks.
All inputs are finite; a program needn't handle non-finite values.
Results may differ from a plain program's by a relative error of at most 0.018.
Values may be sent and summed in bfloat16 or wider, within the bound.
No kernel may reach another device: no remote copies, remote signals or barrier semaphores. Data moves between devices by JAX's collectives and lax.ppermute only.
A program may use at most 128 MiB of HBM per device.

v0:
```python
import jax
import jax.numpy as jnp
from jax import lax
from jax.sharding import PartitionSpec as P

D = 8192
FF = 16384
inv_root_two = 0.7071067811865476
inv_root_tau = 0.3989422804014327


def gelu_parts(values):
    normal_cdf = 0.5 * (1.0 + jax.scipy.special.erf(values * inv_root_two))
    density = inv_root_tau * jnp.exp(-0.5 * values * values)
    return (values * normal_cdf, normal_cdf + values * density)


def grouped_pick(acting, far_index, hidden_blocks, block_size):
    rows_here = acting.shape[0]
    picked = acting.reshape(rows_here, -1, block_size)[:, far_index]
    return picked.reshape(rows_here, hidden_blocks, -1, block_size)


def add_far(product, far_index, model_blocks):
    rows_here = product.shape[0]
    block_size = product.shape[-1]
    flat = product.reshape(rows_here, -1, block_size)
    summed = (
        jnp.zeros((rows_here, model_blocks, block_size), jnp.float32).at[:, far_index].add(flat)
    )
    return summed.reshape(rows_here, model_blocks * block_size)


def grouped_tiles(tiles, order, hidden_blocks):
    block_size = tiles.shape[1]
    return tiles[order].reshape(hidden_blocks, -1, block_size, block_size)


def body(activations, cotangent, up_tiles, down_tiles, up_rows, up_cols, down_rows, down_cols):
    block_size = up_tiles.shape[1]
    hidden_blocks = FF // (block_size * lax.axis_size("tensor"))
    model_blocks = D // block_size
    up_order = jnp.argsort(up_cols[:, 0], stable=True)
    down_order = jnp.argsort(down_rows[:, 0], stable=True)
    up_back = jnp.argsort(up_order)
    down_back = jnp.argsort(down_order)
    up_far = up_rows[:, 0][up_order]
    down_far = down_cols[:, 0][down_order]
    full_input = lax.all_gather(activations, "tensor", axis=1, tiled=True)
    input_pick = grouped_pick(full_input, up_far, hidden_blocks, block_size)
    up_whole = lax.all_gather(up_tiles, "fsdp", axis=0, tiled=True)
    up_sorted = grouped_tiles(up_whole, up_order, hidden_blocks)
    pre_act = jnp.einsum(
        "thkb,hkbc->thc", input_pick, up_sorted, preferred_element_type=jnp.float32
    )
    gelu_out, gelu_slope = gelu_parts(pre_act)
    hidden = gelu_out.astype(jnp.bfloat16)
    down_whole = lax.all_gather(down_tiles, "fsdp", axis=0, tiled=True)
    down_sorted = grouped_tiles(down_whole, down_order, hidden_blocks)
    out_product = jnp.einsum(
        "thb,hkbc->thkc", hidden, down_sorted, preferred_element_type=jnp.float32
    )
    partial_out = add_far(out_product, down_far, model_blocks)
    output = lax.psum_scatter(
        partial_out.astype(jnp.bfloat16), "tensor", scatter_dimension=1, tiled=True
    )
    full_cotangent = lax.all_gather(cotangent, "tensor", axis=1, tiled=True)
    cot_pick = grouped_pick(full_cotangent, down_far, hidden_blocks, block_size)
    hidden_grad = jnp.einsum(
        "thkc,hkbc->thb", cot_pick, down_sorted, preferred_element_type=jnp.float32
    )
    pre_grad = (hidden_grad * gelu_slope).astype(jnp.bfloat16)
    in_product = jnp.einsum(
        "thc,hkbc->thkb", pre_grad, up_sorted, preferred_element_type=jnp.float32
    )
    partial_in = add_far(in_product, up_far, model_blocks)
    input_grad = lax.psum_scatter(
        partial_in.astype(jnp.bfloat16), "tensor", scatter_dimension=1, tiled=True
    )
    up_grouped = jnp.einsum(
        "thkb,thc->hkbc", input_pick, pre_grad, preferred_element_type=jnp.float32
    )
    down_grouped = jnp.einsum(
        "thb,thkc->hkbc", hidden, cot_pick, preferred_element_type=jnp.float32
    )
    up_rounded = up_grouped.astype(jnp.bfloat16).reshape(-1, block_size, block_size)
    down_rounded = down_grouped.astype(jnp.bfloat16).reshape(-1, block_size, block_size)
    up_term = up_rounded[up_back].astype(jnp.float32)
    down_term = down_rounded[down_back].astype(jnp.float32)
    up_part, down_part = (
        lax.psum_scatter(
            up_term.astype(jnp.bfloat16), "fsdp", scatter_dimension=0, tiled=True
        ).astype(jnp.float32),
        lax.psum_scatter(
            down_term.astype(jnp.bfloat16), "fsdp", scatter_dimension=0, tiled=True
        ).astype(jnp.float32),
    )
    up_grad, down_grad = (
        lax.psum(up_part.astype(jnp.bfloat16), "dp").astype(jnp.float32),
        lax.psum(down_part.astype(jnp.bfloat16), "dp").astype(jnp.float32),
    )
    return (output, input_grad, up_grad, down_grad)


def solution(mesh):
    in_specs = (
        P(("dp", "fsdp"), "tensor"),
        P(("dp", "fsdp"), "tensor"),
        P(("fsdp", "tensor"), None, None),
        P(("fsdp", "tensor"), None, None),
        P(None, "tensor"),
        P(None, "tensor"),
        P(None, "tensor"),
        P(None, "tensor"),
    )
    out_specs = (
        P(("dp", "fsdp"), "tensor"),
        P(("dp", "fsdp"), "tensor"),
        P(("fsdp", "tensor"), None, None),
        P(("fsdp", "tensor"), None, None),
    )
    return jax.shard_map(body, mesh=mesh, in_specs=in_specs, out_specs=out_specs, check_vma=False)
```

profile of v0, /device:TPU:1, one launch (start us, length us, event | category | flops | bytes accessed | tf_op | source)
XLA Modules:
  0.0 480.6 jit_solution(9236470539080875752)
XLA Ops:
  7.2 0.0 all-gather.9.cloned.1.call-start
  7.2 1.8 copy.58
  9.0 0.0 all-gather.9.cloned.1.call-update
  9.0 0.0 all-gather.11.cloned.1.call-start
  9.1 1.8 copy.65
  10.9 0.0 all-gather.11.cloned.1.call-update
  10.9 0.0 all-gather.7.cloned.1.call-start
  11.0 0.7 all-gather.7.cloned.1.call-update
  11.7 0.0 all-gather.5.cloned.1.call-start
  11.7 0.5 all-gather.5.cloned.1.call-update
  12.2 0.0 reduce-scatter.9.cloned.1.call-start
  12.3 3.2 sort.63
  15.5 2.5 sort.64
  18.0 1.2 gather_fusion.3
  19.3 3.2 sort.62
  22.5 1.6 gather_fusion
  24.1 28.0 %all-gather.9.cloned.1.call-done = bf16[128,8192]{0,1:T(8,128)(2,1)} async-done(((bf16[128,1024]{0,1:T(8,128)(2,1)}), bf16[128,8192]{0,1:T(8,128)(2,1)}) %all-gather.9.cloned.1.call-update) | async-done | bytes 2097168 | tf_op jit(solution)/shard_map/all_gather | solution.py:49
  52.1 3.2 copy.59
  55.3 39.0 %all-gather.11.cloned.1.call-done = bf16[128,8192]{0,1:T(8,128)(2,1)} async-done(((bf16[128,1024]{0,1:T(8,128)(2,1)}), bf16[128,8192]{0,1:T(8,128)(2,1)}) %all-gather.11.cloned.1.call-update) | async-done | bytes 2097168 | tf_op jit(solution)/shard_map/all_gather | solution.py:67
  94.3 4.1 copy.66
  98.4 3.0 gather_fusion.4
  101.4 4.6 gather_fusion.5
  106.0 32.7 %all-gather.7.cloned.1.call-done = bf16[128,128,128]{2,1,0:T(8,128)(2,1)} async-done(((bf16[8,128,128]{2,1,0:T(8,128)(2,1)}), bf16[128,128,128]{2,1,0:T(8,128)(2,1)}) %all-gather.7.cloned.1.call-update) | async-done | bytes 4194320 | tf_op jit(solution)/shard_map/all_gather | solution.py:51
  138.7 5.2 %gather_fusion.2 = bf16[128,128,128]{2,1,0:T(8,128)(2,1)} fusion(bf16[128,128,128]{2,1,0:T(8,128)(2,1)} %all-gather.7.cloned.1.call-done, s32[1024]{0:T(1024)S(1)} %pad_clamp_fusion.4), kind=kCustom, calls=%fused_computation.2 | custom fusion | bytes 8389120 | tf_op jit(solution)/shard_map/gather | solution.py:36
  143.9 4.8 convolution_bitcast_fusion.1
  148.7 31.7 %all-gather.5.cloned.1.call-done = bf16[128,128,128]{2,1,0:T(8,128)(2,1)} async-done(((bf16[8,128,128]{2,1,0:T(8,128)(2,1)}), bf16[128,128,128]{2,1,0:T(8,128)(2,1)}) %all-gather.5.cloned.1.call-update) | async-done | bytes 4194320 | tf_op jit(solution)/shard_map/all_gather | solution.py:58
  180.5 5.2 %gather_fusion.1 = bf16[128,128,128]{2,1,0:T(8,128)(2,1)} fusion(bf16[128,128,128]{2,1,0:T(8,128)(2,1)} %all-gather.5.cloned.1.call-done, s32[1024]{0:T(1024)S(1)} %pad_clamp_fusion.5), kind=kCustom, calls=%fused_computation.1 | custom fusion | bytes 8389120 | tf_op jit(solution)/shard_map/gather | solution.py:36
  185.7 5.0 %fusion.2 = bf16[128,16,128,1]{0,2,3,1:T(8,128)(2,1)S(1)} fusion(bf16[16,8,128,128]{3,2,1,0:T(8,128)(2,1)} %bitcast.84, bf16[128,16,8,128]{3,0,2,1:T(8,128)(2,1)} %bitcast.86, f32[128,16,128]{0,2,1:T(8,128)S(1)} %convolution_bitcast_fusion.1), kind=kOutput, calls=%fused_computation.17 | convolution fusion | flops 539492352 | bytes 9961472 | tf_op jit(solution)/shard_map/thkc,hkbc->thb/dot_general | solution.py:69
  190.7 3.3 convolution_convert_fusion.1
  194.0 5.2 %gather_fusion.6 = bf16[128,128,128]{2,1,0:T(8,128)(2,1)} fusion(bf16[128,128,128]{2,1,0:T(8,128)(2,1)} %bitcast.88, s32[1024]{0:T(1024)S(1)} %pad_clamp_fusion.1), kind=kCustom, calls=%fused_computation.6 | custom fusion | bytes 8389120 | tf_op jit(solution)/shard_map/gather | solution.py:88
  199.2 0.0 reduce-scatter.9.cloned.1.call-update
  199.2 0.2 reduce-scatter.11.cloned.1.call-start
  199.5 2.5 sort.65
  202.0 5.6 %convolution_convert_fusion = bf16[16,8,128,128]{3,2,1,0:T(8,128)(2,1)} fusion(bf16[128,16,8,128]{3,0,2,1:T(8,128)(2,1)} %bitcast.87, f32[128,16,128]{0,2,1:T(8,128)S(1)} %convolution_bitcast_fusion.1), kind=kOutput, calls=%fused_computation.10 | convolution fusion | flops 540278784 | bytes 9437184 | tf_op jit(solution)/shard_map/thb,thkc->hkbc/dot_general | solution.py:83
  207.6 6.4 %copy.74 = bf16[128,128,128]{2,1,0:T(8,128)(2,1)} copy(bf16[128,128,128]{1,2,0:T(8,128)(2,1)} %bitcast.89) | data formatting | bytes 8388608 | tf_op jit(solution)/shard_map/reshape | solution.py:87
  214.0 5.3 %gather_fusion.7 = bf16[128,128,128]{2,1,0:T(8,128)(2,1)} fusion(bf16[128,128,128]{2,1,0:T(8,128)(2,1)} %copy.74, s32[1024]{0:T(1024)S(1)} %pad_clamp_fusion), kind=kCustom, calls=%fused_computation.7 | custom fusion | bytes 8389120 | tf_op jit(solution)/shard_map/gather | solution.py:89
  219.3 0.0 reduce-scatter.11.cloned.1.call-update
  219.4 0.0 reduce-scatter.7.cloned.1.call-start
  219.4 6.7 %fusion.13 = f32[16,8,128,128]{3,2,1,0:T(8,128)} fusion(bf16[16,8,128,128]{3,2,1,0:T(8,128)(2,1)} %bitcast.77, bf16[128,16,128,1]{0,2,3,1:T(8,128)(2,1)S(1)} %fusion.2), kind=kOutput, calls=%fused_computation.40 | convolution fusion | flops 536870912 | bytes 13107200 | tf_op jit(solution)/shard_map/thc,hkbc->thkb/dot_general | solution.py:73
  226.1 9.0 %copy.68 = f32[128,128,128]{2,0,1:T(8,128)} copy(f32[128,128,128]{0,2,1:T(8,128)} %bitcast.82) | data formatting | bytes 16777216 | tf_op jit(solution)/shard_map/reshape | solution.py:27
  235.1 2.5 broadcast.42.clone.1
  237.6 26.7 %scatter_fusion.1 = f32[128,64,128]{2,0,1:T(8,128)} fusion(f32[128,64,128]{2,0,1:T(8,128)} %broadcast.42.clone.1, s32[128]{0:T(128)S(1)} %fusion.9, f32[128,128,128]{2,1,0:T(8,128)} %bitcast.81), kind=kCustom, calls=%fused_computation.9 | custom fusion | flops 2097152 | bytes 25166336 | tf_op jit(solution)/shard_map/scatter-add | solution.py:29
  264.3 2.6 convert_element_type.45
  266.9 2.9 copy.69
  269.9 0.0 reduce-scatter.7.cloned.1.call-update
  269.9 0.0 reduce-scatter.5.cloned.1.call-start
  270.0 6.8 %fusion.11 = f32[16,8,128,128]{3,2,1,0:T(8,128)} fusion(bf16[16,8,128,128]{3,2,1,0:T(8,128)(2,1)} %bitcast.85, f32[128,16,128]{0,2,1:T(8,128)S(1)} %convolution_bitcast_fusion.1), kind=kOutput, calls=%fused_computation.39 | convolution fusion | flops 538181632 | bytes 13631488 | tf_op jit(solution)/shard_map/thb,hkbc->thkc/dot_general | solution.py:60
  276.7 9.0 %copy.63 = f32[128,128,128]{2,0,1:T(8,128)} copy(f32[128,128,128]{0,2,1:T(8,128)} %bitcast.83) | data formatting | bytes 16777216 | tf_op jit(solution)/shard_map/reshape | solution.py:27
  285.8 2.5 broadcast.42.clone
  288.2 26.9 %scatter_fusion = f32[128,64,128]{2,0,1:T(8,128)} fusion(f32[128,64,128]{2,0,1:T(8,128)} %broadcast.42.clone, s32[128]{0:T(128)S(1)} %fusion.8, f32[128,128,128]{2,1,0:T(8,128)} %bitcast.80), kind=kCustom, calls=%fused_computation.8 | custom fusion | flops 2097152 | bytes 25166336 | tf_op jit(solution)/shard_map/scatter-add | solution.py:29
  315.1 2.6 convert_element_type.42
  317.7 2.9 copy.64
  320.6 0.0 reduce-scatter.5.cloned.1.call-update
  320.7 0.0 all-reduce.3.cloned.1.call-start
  320.7 0.0 reduce-scatter.9.cloned.1.call-done
  320.7 16.4 %reduce-scatter.11.cloned.1.call-done = bf16[8,128,128]{2,1,0:T(8,128)(2,1)} async-done(((bf16[128,128,128]{2,1,0:T(8,128)(2,1)}), bf16[8,128,128]{2,1,0:T(8,128)(2,1)}) %reduce-scatter.11.cloned.1.call-update) | async-done | bytes 262160 | tf_op jit(solution)/shard_map/reduce_scatter | solution.py:94
  337.1 0.0 all-reduce.3.cloned.1.call-update
  337.1 42.2 %reduce-scatter.7.cloned.1.call-done = bf16[128,1024]{0,1:T(8,128)(2,1)} async-done(((bf16[128,8192]{0,1:T(8,128)(2,1)}), bf16[128,1024]{0,1:T(8,128)(2,1)}) %reduce-scatter.7.cloned.1.call-update) | async-done | bytes 262160 | tf_op jit(solution)/shard_map/reduce_scatter | solution.py:77
  379.4 1.8 copy.76
  381.1 41.9 %reduce-scatter.5.cloned.1.call-done = bf16[128,1024]{0,1:T(8,128)(2,1)} async-done(((bf16[128,8192]{0,1:T(8,128)(2,1)}), bf16[128,1024]{0,1:T(8,128)(2,1)}) %reduce-scatter.5.cloned.1.call-update) | async-done | bytes 262160 | tf_op jit(solution)/shard_map/reduce_scatter | solution.py:64
  423.0 1.8 copy.75
  424.8 45.7 %all-reduce.3.cloned.1.call-done = (bf16[8,128,128]{2,1,0:T(8,128)(2,1)}, bf16[8,128,128]{2,1,0:T(8,128)(2,1)}) async-done(((bf16[8,128,128]{2,1,0:T(8,128)(2,1)}, bf16[8,128,128]{2,1,0:T(8,128)(2,1)}), (bf16[8,128,128]{2,1,0:T(8,128)(2,1)}, bf16[8,128,128]{2,1,0:T(8,128)(2,1)})) %all-reduce.3.cloned.1.call-update) | async-done | bytes 524304 | tf_op jit(solution)/shard_map/psum | solution.py:99
  470.5 1.8 convert_element_type.48
  472.3 1.8 convert_element_type.51
  (22 shorter events, 0.1 us)
Async XLA Ops:
  7.2 10.9 %copy-start = (s32[128,1]{0,1:T(1,128)S(1)}, s32[128,1]{0,1:T(1,128)}, u32[]{:S(2)}) copy-start(s32[128,1]{0,1:T(1,128)} %param.12) | copy-start | bytes 1540
  7.2 44.9 %all-gather.9.cloned.1.call-start = ((), (), s32[]{:S(2)}) async-start(), calls=%async_computation.6 | async-start | bytes 2359296 | tf_op jit(solution)/shard_map/all_gather | solution.py:49
  9.0 85.3 %all-gather.11.cloned.1.call-start = ((), (), s32[]{:S(2)}) async-start(), calls=%async_computation.8 | async-start | bytes 2359296 | tf_op jit(solution)/shard_map/all_gather | solution.py:67
  10.9 127.8 %all-gather.7.cloned.1.call-start = ((), (), s32[]{:S(2)}) async-start(), calls=%async_computation.5 | async-start | bytes 4456448 | tf_op jit(solution)/shard_map/all_gather | solution.py:51
  11.7 168.8 %all-gather.5.cloned.1.call-start = ((), (), s32[]{:S(2)}) async-start(), calls=%async_computation.4 | async-start | bytes 4456448 | tf_op jit(solution)/shard_map/all_gather | solution.py:58
  12.2 308.5 %reduce-scatter.9.cloned.1.call-start = ((), (), s32[]{:S(2)}) async-start(), calls=%async_computation.10 | async-start | bytes 4456448 | tf_op jit(solution)/shard_map/reduce_scatter | solution.py:91
  185.7 5.0 %copy-start.2 = (bf16[128,128,128]{2,1,0:T(8,128)(2,1)S(1)}, bf16[128,128,128]{2,1,0:T(8,128)(2,1)}, u32[]{:S(2)}) copy-start(bf16[128,128,128]{2,1,0:T(8,128)(2,1)} %gather_fusion.4) | copy-start | bytes 12582916
  199.2 137.9 %reduce-scatter.11.cloned.1.call-start = ((), (), s32[]{:S(2)}) async-start(), calls=%async_computation.11 | async-start | bytes 4456448 | tf_op jit(solution)/shard_map/reduce_scatter | solution.py:94
  219.4 160.0 %reduce-scatter.7.cloned.1.call-start = ((), (), s32[]{:S(2)}) async-start(), calls=%async_computation.9 | async-start | bytes 2359296 | tf_op jit(solution)/shard_map/reduce_scatter | solution.py:77
  269.9 153.1 %reduce-scatter.5.cloned.1.call-start = ((), (), s32[]{:S(2)}) async-start(), calls=%async_computation.7 | async-start | bytes 2359296 | tf_op jit(solution)/shard_map/reduce_scatter | solution.py:64
  315.1 158.9 %copy-start.1 = (s32[128,1]{0,1:T(1,128)S(1)}, s32[128,1]{0,1:T(1,128)}, u32[]{:S(2)}) copy-start(s32[128,1]{0,1:T(1,128)} %param.12) | copy-start | bytes 1540
  320.7 149.9 %all-reduce.3.cloned.1.call-start = ((), (), s32[]{:S(2)}) async-start(), calls=%async_computation.12 | async-start | bytes 1048576 | tf_op jit(solution)/shard_map/psum | solution.py:99
Sparse Core Ops, SparseCore 0:
  10.4 41.6 all-gather.8
  54.5 39.8 all-gather.10
  96.2 42.5 all-gather.6
  140.4 39.9 all-gather.4
  199.3 66.5 reduce-scatter.8
  268.4 68.6 reduce-scatter.10
  339.7 39.6 reduce-scatter.6
  381.9 41.0 reduce-scatter.4
  425.7 44.8 all-reduce.2
where the time goes:
time: 482 us; the launch traced here: 481 us
  waiting for transfers between devices  279 us (58%)
  local copies, waits for them, and re-layouts  81.1 us (17%)
  other arithmetic  73.8 us (15%)
  matrix products  32.2 us (7%)
  between operations  14 us (3%)
    scatter-add x2, other arithmetic, add_far(): jnp.zeros((rows_here, model_blocks, block_size), jnp.float32)  53.6 us
    psum x1, waiting for transfers between devices, body(): lax.psum(up_part.astype(jnp.bfloat16), 'dp').astype(jnp.float32)  45.7 us
    reduce_scatter x1, waiting for transfers between devices, body(): lax.psum_scatter(partial_in.astype(jnp.bfloat16), 'tensor', scatter_dimen...  42.2 us
    reduce_scatter x1, waiting for transfers between devices, body(): lax.psum_scatter(partial_out.astype(jnp.bfloat16), 'tensor', scatter_dime...  41.9 us
    all_gather x1, waiting for transfers between devices, body(): full_cotangent = lax.all_gather(cotangent, 'tensor', axis=1, tiled=True)  39 us
    all_gather x1, waiting for transfers between devices, body(): up_whole = lax.all_gather(up_tiles, 'fsdp', axis=0, tiled=True)  32.7 us
    all_gather x1, waiting for transfers between devices, body(): down_whole = lax.all_gather(down_tiles, 'fsdp', axis=0, tiled=True)  31.7 us
    all_gather x1, waiting for transfers between devices, body(): full_input = lax.all_gather(activations, 'tensor', axis=1, tiled=True)  28 us
  transfers between devices with their start and end apart: 9, of which 8 were waited for; matrix products, arithmetic and copies ran while one was open for 34% of the time, Pallas kernels for 0%

commit v1 on v0

--- a/solution.py
+++ b/solution.py
@@ -1,3 +1,4 @@
+import functools
 import jax
 import jax.numpy as jnp
 from jax import lax
@@ -7,6 +8,13 @@
 FF = 16384
 inv_root_two = 0.7071067811865476
 inv_root_tau = 0.3989422804014327
+
+
+def _launch_columns(state, axis_name):
+    return lax.all_gather(state, axis_name).sum(axis=0)
+
+
+_place_stocks = functools.partial(_launch_columns, axis_name="dp")
 
 
 def gelu_parts(values):
@@ -96,7 +104,7 @@
         ).astype(jnp.float32),
     )
     up_grad, down_grad = (
-        lax.psum(up_part.astype(jnp.bfloat16), "dp").astype(jnp.float32),
+        _place_stocks(up_part.astype(jnp.bfloat16)).astype(jnp.float32),
         lax.psum(down_part.astype(jnp.bfloat16), "dp").astype(jnp.float32),
     )
     return (output, input_grad, up_grad, down_grad)

time: 482 us -> 457 us (0.948)
  waiting for transfers between devices: 279 us -> 249 us
  blocking collectives: 0 us -> 7.6 us
    reduce_scatter x1, waiting for transfers between devices: 0.02 us -> 70.8 us  [body(): lax.psum_scatter(up_term.astype(jnp.bfloat16), 'fsdp', scatter_dimension=...]
    reduce_scatter x1, waiting for transfers between devices: 41.9 us -> 0.02 us  [body(): lax.psum_scatter(partial_out.astype(jnp.bfloat16), 'tensor', scatter_dime...]
    reduce_scatter x1, waiting for transfers between devices: 16.4 us -> 0.02 us  [body(): lax.psum_scatter(down_term.astype(jnp.bfloat16), 'fsdp', scatter_dimensio...]
    all_gather x1, waiting for transfers between devices: 31.7 us -> 16.1 us  [body(): down_whole = lax.all_gather(down_tiles, 'fsdp', axis=0, tiled=True)]
    psum x1, waiting for transfers between devices: 45.7 us -> 31.8 us  [body(): lax.psum(down_part.astype(jnp.bfloat16), 'dp').astype(jnp.float32)]
    reduce_scatter x1, waiting for transfers between devices: 42.2 us -> 29.3 us  [body(): lax.psum_scatter(partial_in.astype(jnp.bfloat16), 'tensor', scatter_dimen...]
    all_gather x0 -> x1, blocking collectives: none -> 7.6 us  [_launch_columns(): return lax.all_gather(state, axis_name).sum(axis=0)]
  transfers between devices with their start and end apart: 9 -> 9, of which waited for: 8 -> 7; matrix products, arithmetic and copies ran while one was open for 34% -> 40% of each run, Pallas kernels for 0% -> 0%
where the time goes in v1:
time: 457 us; the launch traced here: 456 us
  waiting for transfers between devices  249 us (54%)
  local copies, waits for them, and re-layouts  81.3 us (18%)
  other arithmetic  72.9 us (16%)
  matrix products  30.2 us (7%)
  between operations  14 us (3%)
  blocking collectives  7.6 us (2%)
    reduce_scatter x1, waiting for transfers between devices, body(): lax.psum_scatter(up_term.astype(jnp.bfloat16), 'fsdp', scatter_dimension=...  70.8 us
    scatter-add x2, other arithmetic, add_far(): jnp.zeros((rows_here, model_blocks, block_size), jnp.float32)  53.5 us
    all_gather x1, waiting for transfers between devices, body(): full_cotangent = lax.all_gather(cotangent, 'tensor', axis=1, tiled=True)  38.8 us
    all_gather x1, waiting for transfers between devices, body(): up_whole = lax.all_gather(up_tiles, 'fsdp', axis=0, tiled=True)  32.7 us
    psum x1, waiting for transfers between devices, body(): lax.psum(down_part.astype(jnp.bfloat16), 'dp').astype(jnp.float32)  31.8 us
    reduce_scatter x1, waiting for transfers between devices, body(): lax.psum_scatter(partial_in.astype(jnp.bfloat16), 'tensor', scatter_dimen...  29.3 us
    all_gather x1, waiting for transfers between devices, body(): full_input = lax.all_gather(activations, 'tensor', axis=1, tiled=True)  27.5 us
    reshape x2, local copies, waits for them, and re-layouts, add_far(): flat = product.reshape(rows_here, -1, block_size)  18.1 us
  transfers between devices with their start and end apart: 9, of which 7 were waited for; matrix products, arithmetic and copies ran while one was open for 40% of the time, Pallas kernels for 0%

profile of v1, /device:TPU:1, one launch (start us, length us, event | category | flops | bytes accessed | tf_op | source)
XLA Modules:
  0.0 455.7 jit_solution(8221388175862385165)
XLA Ops:
  7.2 0.0 all-gather.10.cloned.1.call-start
  7.2 1.8 copy.58
  9.0 0.0 all-gather.10.cloned.1.call-update
  9.0 0.0 all-gather.12.cloned.1.call-start
  9.1 1.8 copy.65
  10.9 0.0 all-gather.12.cloned.1.call-update
  10.9 0.0 all-gather.8.cloned.1.call-start
  11.0 0.7 all-gather.8.cloned.1.call-update
  11.7 0.0 all-gather.6.cloned.1.call-start
  11.7 0.5 all-gather.6.cloned.1.call-update
  12.2 0.0 reduce-scatter.11.cloned.1.call-start
  12.3 3.2 sort.62
  15.5 2.5 sort.65
  18.0 3.2 sort.63
  21.2 1.2 gather_fusion.3
  22.5 1.6 gather_fusion
  24.1 27.5 %all-gather.10.cloned.1.call-done = bf16[128,8192]{0,1:T(8,128)(2,1)} async-done(((bf16[128,1024]{0,1:T(8,128)(2,1)}), bf16[128,8192]{0,1:T(8,128)(2,1)}) %all-gather.10.cloned.1.call-update) | async-done | bytes 2097168 | tf_op jit(solution)/shard_map/all_gather | solution.py:57
  51.6 3.2 copy.59
  54.8 38.8 %all-gather.12.cloned.1.call-done = bf16[128,8192]{0,1:T(8,128)(2,1)} async-done(((bf16[128,1024]{0,1:T(8,128)(2,1)}), bf16[128,8192]{0,1:T(8,128)(2,1)}) %all-gather.12.cloned.1.call-update) | async-done | bytes 2097168 | tf_op jit(solution)/shard_map/all_gather | solution.py:75
  93.7 4.1 copy.66
  97.7 4.6 %gather_fusion.5 = bf16[128,128,128]{2,1,0:T(8,128)(2,1)} fusion(bf16[128,64,128]{2,0,1:T(8,128)(2,1)} %copy.66, s32[1024]{0:T(1024)S(1)} %pad_clamp_fusion.2), kind=kCustom, calls=%fused_computation.5 | custom fusion | bytes 8389120 | tf_op jit(solution)/shard_map/gather | solution.py:28
  102.4 3.0 gather_fusion.4
  105.4 32.7 %all-gather.8.cloned.1.call-done = bf16[128,128,128]{2,1,0:T(8,128)(2,1)} async-done(((bf16[8,128,128]{2,1,0:T(8,128)(2,1)}), bf16[128,128,128]{2,1,0:T(8,128)(2,1)}) %all-gather.8.cloned.1.call-update) | async-done | bytes 4194320 | tf_op jit(solution)/shard_map/all_gather | solution.py:59
  138.1 5.2 %gather_fusion.2 = bf16[128,128,128]{2,1,0:T(8,128)(2,1)} fusion(bf16[128,128,128]{2,1,0:T(8,128)(2,1)} %all-gather.8.cloned.1.call-done, s32[1024]{0:T(1024)S(1)} %pad_clamp_fusion.4), kind=kCustom, calls=%fused_computation.2 | custom fusion | bytes 8389120 | tf_op jit(solution)/shard_map/gather | solution.py:44
  143.3 4.9 %convolution_bitcast_fusion.1 = f32[128,16,128]{0,2,1:T(8,128)S(1)} fusion(bf16[16,8,128,128]{3,2,1,0:T(8,128)(2,1)} %bitcast.77, bf16[128,16,8,128]{3,0,2,1:T(8,128)(2,1)} %bitcast.79), kind=kOutput, calls=%fused_computation.14 | convolution fusion | flops 536870912 | bytes 9437184 | tf_op jit(solution)/shard_map/thkb,hkbc->thc/dot_general | solution.py:61
  148.3 3.5 convolution_convert_fusion
  151.7 6.4 %copy.74 = bf16[128,128,128]{2,1,0:T(8,128)(2,1)} copy(bf16[128,128,128]{1,2,0:T(8,128)(2,1)} %bitcast.90) | data formatting | bytes 8388608 | tf_op jit(solution)/shard_map/reshape | solution.py:95
  158.1 5.3 %gather_fusion.7 = bf16[128,128,128]{2,1,0:T(8,128)(2,1)} fusion(bf16[128,128,128]{2,1,0:T(8,128)(2,1)} %copy.74, s32[1024]{0:T(1024)S(1)} %pad_clamp_fusion), kind=kCustom, calls=%fused_computation.7 | custom fusion | bytes 8389120 | tf_op jit(solution)/shard_map/gather | solution.py:97
  163.4 0.0 reduce-scatter.11.cloned.1.call-update
  163.5 0.2 reduce-scatter.5.cloned.1.call-start
  163.7 16.1 %all-gather.6.cloned.1.call-done = bf16[128,128,128]{2,1,0:T(8,128)(2,1)} async-done(((bf16[8,128,128]{2,1,0:T(8,128)(2,1)}), bf16[128,128,128]{2,1,0:T(8,128)(2,1)}) %all-gather.6.cloned.1.call-update) | async-done | bytes 4194320 | tf_op jit(solution)/shard_map/all_gather | solution.py:66
  179.8 5.3 %gather_fusion.1 = bf16[128,128,128]{2,1,0:T(8,128)(2,1)} fusion(bf16[128,128,128]{2,1,0:T(8,128)(2,1)} %all-gather.6.cloned.1.call-done, s32[1024]{0:T(1024)S(1)} %pad_clamp_fusion.5), kind=kCustom, calls=%fused_computation.1 | custom fusion | bytes 8389120 | tf_op jit(solution)/shard_map/gather | solution.py:44
  185.1 6.8 %fusion.11 = f32[16,8,128,128]{3,2,1,0:T(8,128)} fusion(bf16[16,8,128,128]{3,2,1,0:T(8,128)(2,1)} %bitcast.87, f32[128,16,128]{0,2,1:T(8,128)S(1)} %convolution_bitcast_fusion.1), kind=kOutput, calls=%fused_computation.39 | convolution fusion | flops 538181632 | bytes 13631488 | tf_op jit(solution)/shard_map/thb,hkbc->thkc/dot_general | solution.py:68
  191.9 9.0 %copy.63 = f32[128,128,128]{2,0,1:T(8,128)} copy(f32[128,128,128]{0,2,1:T(8,128)} %bitcast.84) | data formatting | bytes 16777216 | tf_op jit(solution)/shard_map/reshape | solution.py:35
  201.0 2.5 broadcast.42.clone
  203.4 26.9 %scatter_fusion = f32[128,64,128]{2,0,1:T(8,128)} fusion(f32[128,64,128]{2,0,1:T(8,128)} %broadcast.42.clone, s32[128]{0:T(128)S(1)} %fusion.8, f32[128,128,128]{2,1,0:T(8,128)} %bitcast.82), kind=kCustom, calls=%fused_computation.8 | custom fusion | flops 2097152 | bytes 25166336 | tf_op jit(solution)/shard_map/scatter-add | solution.py:37
  230.3 2.6 convert_element_type.44
  232.9 2.9 copy.64
  235.8 0.0 reduce-scatter.5.cloned.1.call-update
  235.8 0.0 reduce-scatter.7.cloned.1.call-start
  235.9 5.1 %fusion.2 = bf16[128,16,128,1]{0,2,3,1:T(8,128)(2,1)S(1)} fusion(bf16[16,8,128,128]{3,2,1,0:T(8,128)(2,1)} %bitcast.88, bf16[128,16,8,128]{3,0,2,1:T(8,128)(2,1)} %bitcast.85, f32[128,16,128]{0,2,1:T(8,128)S(1)} %convolution_bitcast_fusion.1), kind=kOutput, calls=%fused_computation.17 | convolution fusion | flops 539492352 | bytes 9961472 | tf_op jit(solution)/shard_map/thkc,hkbc->thb/dot_general | solution.py:77
  241.0 4.5 fusion.13
  245.4 9.0 %copy.68 = f32[128,128,128]{2,0,1:T(8,128)} copy(f32[128,128,128]{0,2,1:T(8,128)} %bitcast.83) | data formatting | bytes 16777216 | tf_op jit(solution)/shard_map/reshape | solution.py:35
  254.5 2.5 broadcast.42.clone.1
  256.9 26.6 %scatter_fusion.1 = f32[128,64,128]{2,0,1:T(8,128)} fusion(f32[128,64,128]{2,0,1:T(8,128)} %broadcast.42.clone.1, s32[128]{0:T(128)S(1)} %fusion.9, f32[128,128,128]{2,1,0:T(8,128)} %bitcast.81), kind=kCustom, calls=%fused_computation.9 | custom fusion | flops 2097152 | bytes 25166336 | tf_op jit(solution)/shard_map/scatter-add | solution.py:37
  283.6 2.6 convert_element_type.47
  286.2 3.0 copy.69
  289.2 0.0 reduce-scatter.9.cloned.1.call-start
  289.2 2.5 sort.64
  291.8 5.5 %convolution_convert_fusion.1 = bf16[16,8,128,128]{3,2,1,0:T(8,128)(2,1)} fusion(bf16[128,16,8,128]{3,0,2,1:T(8,128)(2,1)} %bitcast.80, bf16[128,16,128,1]{0,2,3,1:T(8,128)(2,1)S(1)} %fusion.2), kind=kOutput, calls=%fused_computation.11 | convolution fusion | flops 538968064 | bytes 8912896 | tf_op jit(solution)/shard_map/thkb,thc->hkbc/dot_general | solution.py:88
  297.3 5.2 %gather_fusion.6 = bf16[128,128,128]{2,1,0:T(8,128)(2,1)} fusion(bf16[128,128,128]{2,1,0:T(8,128)(2,1)} %bitcast.89, s32[1024]{0:T(1024)S(1)} %pad_clamp_fusion.1), kind=kCustom, calls=%fused_computation.6 | custom fusion | bytes 8389120 | tf_op jit(solution)/shard_map/gather | solution.py:96
  302.5 0.0 all-reduce.2.cloned.1.call-start
  302.6 0.0 reduce-scatter.11.cloned.1.call-done
  302.6 0.7 all-reduce.2.cloned.1.call-update
  303.3 0.0 reduce-scatter.5.cloned.1.call-done
  303.3 1.8 copy.75
  305.1 29.3 %reduce-scatter.7.cloned.1.call-done = bf16[128,1024]{0,1:T(8,128)(2,1)} async-done(((bf16[128,8192]{0,1:T(8,128)(2,1)}), bf16[128,1024]{0,1:T(8,128)(2,1)}) %reduce-scatter.7.cloned.1.call-update) | async-done | bytes 262160 | tf_op jit(solution)/shard_map/reduce_scatter | solution.py:85
  334.4 1.8 copy.76
  336.2 70.8 %reduce-scatter.9.cloned.1.call-done = bf16[8,128,128]{2,1,0:T(8,128)(2,1)} async-done(((bf16[128,128,128]{2,1,0:T(8,128)(2,1)}), bf16[8,128,128]{2,1,0:T(8,128)(2,1)}) %reduce-scatter.9.cloned.1.call-update) | async-done | bytes 262160 | tf_op jit(solution)/shard_map/reduce_scatter | solution.py:99
  407.0 7.6 %all-gather = bf16[16,128,128]{2,1,0:T(8,128)(2,1)S(1)} all-gather(bf16[8,128,128]{2,1,0:T(8,128)(2,1)} %reduce-scatter.9.cloned.1.call-done), channel_id=2, replica_groups=mesh['dp'=2,'fsdp'=16,'tensor'=8] {'dp'}, dimensions={0}, use_global_device_ids=true | all-gather | bytes 786432 | tf_op jit(solution)/shard_map/all_gather | solution.py:14
  414.6 0.1 reduce_sum.12
  414.8 0.8 convert_element_type.50
  415.6 31.8 %all-reduce.2.cloned.1.call-done = bf16[8,128,128]{2,1,0:T(8,128)(2,1)} async-done(((bf16[8,128,128]{2,1,0:T(8,128)(2,1)}), bf16[8,128,128]{2,1,0:T(8,128)(2,1)}) %all-reduce.2.cloned.1.call-update) | async-done | bytes 262160 | tf_op jit(solution)/shard_map/psum | solution.py:108
  447.4 1.8 convert_element_type.53
  (26 shorter events, 0.1 us)
Async XLA Ops:
  7.2 14.0 %copy-start = (s32[128,1]{0,1:T(1,128)S(1)}, s32[128,1]{0,1:T(1,128)}, u32[]{:S(2)}) copy-start(s32[128,1]{0,1:T(1,128)} %param.12) | copy-start | bytes 1540
  7.2 44.4 %all-gather.10.cloned.1.call-start = ((), (), s32[]{:S(2)}) async-start(), calls=%async_computation.6 | async-start | bytes 2359296 | tf_op jit(solution)/shard_map/all_gather | solution.py:57
  9.0 84.6 %all-gather.12.cloned.1.call-start = ((), (), s32[]{:S(2)}) async-start(), calls=%async_computation.8 | async-start | bytes 2359296 | tf_op jit(solution)/shard_map/all_gather | solution.py:75
  10.9 127.2 %all-gather.8.cloned.1.call-start = ((), (), s32[]{:S(2)}) async-start(), calls=%async_computation.5 | async-start | bytes 4456448 | tf_op jit(solution)/shard_map/all_gather | solution.py:59
  11.7 168.2 %all-gather.6.cloned.1.call-start = ((), (), s32[]{:S(2)}) async-start(), calls=%async_computation.4 | async-start | bytes 4456448 | tf_op jit(solution)/shard_map/all_gather | solution.py:66
  12.2 290.4 %reduce-scatter.11.cloned.1.call-start = ((), (), s32[]{:S(2)}) async-start(), calls=%async_computation.11 | async-start | bytes 4456448 | tf_op jit(solution)/shard_map/reduce_scatter | solution.py:102
  143.3 4.9 %copy-start.3 = (bf16[128,128,128]{2,1,0:T(8,128)(2,1)S(1)}, bf16[128,128,128]{2,1,0:T(8,128)(2,1)}, u32[]{:S(2)}) copy-start(bf16[128,128,128]{2,1,0:T(8,128)(2,1)} %gather_fusion.5) | copy-start | bytes 12582916
  163.5 139.8 %reduce-scatter.5.cloned.1.call-start = ((), (), s32[]{:S(2)}) async-start(), calls=%async_computation.7 | async-start | bytes 2359296 | tf_op jit(solution)/shard_map/reduce_scatter | solution.py:72
  235.8 98.6 %reduce-scatter.7.cloned.1.call-start = ((), (), s32[]{:S(2)}) async-start(), calls=%async_computation.9 | async-start | bytes 2359296 | tf_op jit(solution)/shard_map/reduce_scatter | solution.py:85
  235.9 5.1 %copy-start.2 = (bf16[128,128,128]{2,1,0:T(8,128)(2,1)S(1)}, bf16[128,128,128]{2,1,0:T(8,128)(2,1)}, u32[]{:S(2)}) copy-start(bf16[128,128,128]{2,1,0:T(8,128)(2,1)} %gather_fusion.2) | copy-start | bytes 12582916
  289.2 117.9 %reduce-scatter.9.cloned.1.call-start = ((), (), s32[]{:S(2)}) async-start(), calls=%async_computation.10 | async-start | bytes 4456448 | tf_op jit(solution)/shard_map/reduce_scatter | solution.py:99
  302.5 146.6 %copy-start.1 = (s32[128,1]{0,1:T(1,128)S(1)}, s32[128,1]{0,1:T(1,128)}, u32[]{:S(2)}) copy-start(s32[128,1]{0,1:T(1,128)} %param.12) | copy-start | bytes 1540
  302.5 144.8 %all-reduce.2.cloned.1.call-start = ((), (), s32[]{:S(2)}) async-start(), calls=%async_computation.12 | async-start | bytes 524288 | tf_op jit(solution)/shard_map/psum | solution.py:108
Sparse Core Ops, SparseCore 0:
  10.4 41.1 all-gather.9
  54.0 39.6 all-gather.11
  95.5 42.5 all-gather.7
  139.8 39.9 all-gather.5
  182.2 66.5 reduce-scatter.10
  251.2 39.6 reduce-scatter.4
  293.5 40.8 reduce-scatter.6
  337.0 70.0 reduce-scatter.8
  409.6 37.7 all-reduce.1
